TPU v7x, 128 devices: a whole 4x4x4 slice. The times are simulated.
128 devices in a mesh: section: 4 (over y), dp: 32 (over x, z, core).
Axes of the slice: x: 4, y: 4, z: 4, core: 2. Of those that a mesh axis runs over, the one named last changes fastest.
Arguments:
- tokens: bfloat16 [8192, 4096], P('dp'), may hold values from -6 to 6
- cotangent: bfloat16 [8192, 4096], P('dp'), may hold values from -30 to 30
- lengths: int32 [128], P('dp'), may hold values from 1 to 64
- seq_user: int32 [128], P('dp'), may hold values from 0 to 63, as said below
- norm_gains: float32 [4, 4096], P('section'), may hold values from 0.5 to 1.5
- weights: float32 [4, 4096, 2, 256], P('section', 'dp'), may hold values from -1 to 1
- first_moment: float32 [4, 4096, 2, 256], P('section', 'dp'), may hold values from -6 to 6
- second_moment: float32 [4, 4096, 2, 256], P('section', 'dp'), may hold values from 0.25 to 4
Outputs:
- new_first: float32 [4, 4096, 2, 256], P('section', 'dp')
- new_second: float32 [4, 4096, 2, 256], P('section', 'dp')
- step_dir: float32 [4, 4096, 2, 256], P('section', 'dp')
- user_ratio: float32 [64], P('dp')
Inputs may be any that keep to these rules, and one draw needn't show every extreme that they name: `seq_user`: the i-th block of 4 sequences carries only the user ids i * 2 to i * 2 + 1, each of them at least once.
All inputs are finite; a program needn't handle non-finite values.
Results may differ from a plain program's by a relative error of at most 0.0045.
Values may be sent and summed in bfloat16 or wider, within the bound.
No kernel may reach another device: no remote copies, remote signals or barrier semaphores. Data moves between devices by JAX's collectives and lax.ppermute only.
A program may use at most 128 MiB of HBM per device.

v0:
```python
import jax
import jax.numpy as jnp
from jax import lax
from jax.sharding import PartitionSpec as P

SEQLEN = 64
USERS_DEV = 2
CLIP_BOUND = 70000.0
LOSS_SCALE = 1024.0
BETA_ONE = 0.9
BETA_TWO = 0.999
FIRST_FIX = 1.0 - 0.9**50
SECOND_FIX = 1.0 - 0.999**50
ADAM_EPS = 1e-08
NORM_EPS = 1e-05


def passed_along(value, axis, steps):
    count = lax.axis_size(axis)
    initial, last = (max(0, -steps), min(count, count - steps))
    return lax.ppermute(value, axis, [(source, source + steps) for source in range(initial, last)])


def section_forward(hidden, section_gain, down_cast, up_cast):
    widened = hidden.astype(jnp.float32)
    inverse = lax.rsqrt(jnp.mean(widened * widened, axis=-1, keepdims=True) + NORM_EPS)
    normed = (widened * inverse * section_gain).astype(jnp.bfloat16)
    inner_act = jnp.dot(normed, down_cast, preferred_element_type=jnp.float32)
    active = jax.nn.silu(inner_act).astype(jnp.bfloat16)
    branch = lax.dot_general(
        active, up_cast, (((1,), (1,)), ((), ())), preferred_element_type=jnp.float32
    )
    return ((widened + branch).astype(jnp.bfloat16), (widened, inverse, normed, inner_act, active))


def section_backward(grad_out, section_gain, down_cast, up_cast, kept_acts):
    widened, inverse, normed, inner_act, active = kept_acts
    grad_active = jnp.dot(grad_out, up_cast, preferred_element_type=jnp.float32)
    sigmoid_val = jax.nn.sigmoid(inner_act)
    grad_inner = (grad_active * sigmoid_val * (1.0 + inner_act * (1.0 - sigmoid_val))).astype(
        jnp.bfloat16
    )
    grad_normed = lax.dot_general(
        grad_inner, down_cast, (((1,), (1,)), ((), ())), preferred_element_type=jnp.float32
    )
    scaled = grad_normed * section_gain
    projected = jnp.mean(scaled * widened, axis=-1, keepdims=True)
    grad_in = (
        grad_out.astype(jnp.float32)
        + inverse * scaled
        - widened * inverse * inverse * inverse * projected
    )
    return (grad_in.astype(jnp.bfloat16), grad_inner)


def gram_of(values):
    return lax.dot_general(
        values, values, (((1,), (1,)), ((), ())), preferred_element_type=jnp.float32
    )


def user_squares(normed, grad_inner, active, grad_out, owners):
    joint = gram_of(normed) * gram_of(grad_inner) + gram_of(active) * gram_of(grad_out)
    spread = jnp.dot(joint, owners, precision=lax.Precision.HIGHEST)
    return jnp.sum(spread * owners, axis=0)


def keep_block(stored, produced, block_slot, blocks):
    usable = (block_slot >= 0) & (block_slot < blocks)
    clamped = jnp.clip(block_slot, 0, blocks - 1)
    if stored is None:
        stored = tuple(
            (jnp.zeros((blocks,) + element.shape, element.dtype) for element in produced)
        )
    updated = []
    for buffer, element in zip(stored, produced):
        before = lax.dynamic_index_in_dim(buffer, clamped, 0, keepdims=False)
        updated.append(
            lax.dynamic_update_index_in_dim(buffer, jnp.where(usable, element, before), clamped, 0)
        )
    return tuple(updated)


def active_width(stored):
    return stored[4].shape[-1]


def on_device(
    tokens, cotangent, lengths, seq_user, norm_gains, weights, first_moment, second_moment
):
    section_count = lax.axis_size("section")
    section_index = lax.axis_index("section")
    blocks = 1
    tok_rows = tokens.shape[0]
    model_width = tokens.shape[1]
    block_rows = tok_rows // blocks
    rounds = blocks + section_count - 1
    section_gain = norm_gains[0]
    packed = lax.all_gather(weights.astype(jnp.bfloat16), "dp", axis=1, tiled=True)
    down_cast = packed[0, :, 0, :]
    up_cast = packed[0, :, 1, :]
    inputs = tokens.reshape(blocks, block_rows, model_width)
    carried = jnp.zeros((block_rows, model_width), jnp.bfloat16)
    stored = None
    for step_no in range(rounds):
        incoming = jnp.where(section_index == 0, inputs[min(step_no, blocks - 1)], carried)
        result, kept_acts = section_forward(incoming, section_gain, down_cast, up_cast)
        stored = keep_block(stored, kept_acts, step_no - section_index, blocks)
        if step_no + 1 < rounds:
            carried = passed_along(result, "section", 1)
    positions = jnp.arange(tok_rows) % SEQLEN
    usable = positions < jnp.repeat(lengths, SEQLEN)
    local_user = seq_user - lax.axis_index("dp") * USERS_DEV
    token_user = jnp.repeat(local_user, SEQLEN)
    owners = ((token_user[:, None] == jnp.arange(USERS_DEV)[None, :]) & usable[:, None]).astype(
        jnp.float32
    )
    seed_rows = (cotangent * usable[:, None].astype(jnp.bfloat16)).reshape(
        blocks, block_rows, model_width
    )
    carried = jnp.zeros((block_rows, model_width), jnp.bfloat16)
    grad_store = None
    for step_no in range(rounds):
        block_slot = step_no - (section_count - 1 - section_index)
        clamped = jnp.clip(block_slot, 0, blocks - 1)
        incoming = jnp.where(
            section_index == section_count - 1, seed_rows[min(step_no, blocks - 1)], carried
        )
        kept_acts = tuple(
            (lax.dynamic_index_in_dim(buffer, clamped, 0, keepdims=False) for buffer in stored)
        )
        grad_in, grad_inner = section_backward(
            incoming, section_gain, down_cast, up_cast, kept_acts
        )
        grad_store = keep_block(grad_store, (incoming, grad_inner), block_slot, blocks)
        if step_no + 1 < rounds:
            carried = passed_along(grad_in, "section", -1)
    normed_all = stored[2].reshape(tok_rows, model_width)
    active_all = stored[4].reshape(tok_rows, active_width(stored))
    grad_out_all = grad_store[0].reshape(tok_rows, model_width)
    grad_inner_all = grad_store[1].reshape(tok_rows, active_width(stored))
    local_squares = user_squares(normed_all, grad_inner_all, active_all, grad_out_all, owners)
    squares = lax.psum(local_squares, "section")
    user_norm = jnp.sqrt(squares)
    factors = LOSS_SCALE / jnp.maximum(user_norm, CLIP_BOUND)
    token_factor = jnp.dot(owners, factors, precision=lax.Precision.HIGHEST)
    weighted_inner = (grad_inner_all.astype(jnp.float32) * token_factor[:, None]).astype(
        jnp.bfloat16
    )
    weighted_out = (grad_out_all.astype(jnp.float32) * token_factor[:, None]).astype(jnp.bfloat16)
    down_term = lax.dot_general(
        normed_all, weighted_inner, (((0,), (0,)), ((), ())), preferred_element_type=jnp.float32
    )
    up_term = lax.dot_general(
        weighted_out, active_all, (((0,), (0,)), ((), ())), preferred_element_type=jnp.float32
    )
    gradient = lax.psum_scatter(
        jnp.stack([down_term, up_term], axis=1).astype(jnp.bfloat16),
        "dp",
        scatter_dimension=0,
        tiled=True,
    ).astype(jnp.float32)
    moment_one = BETA_ONE * first_moment[0] + (1.0 - BETA_ONE) * gradient
    moment_two = BETA_TWO * second_moment[0] + (1.0 - BETA_TWO) * gradient * gradient
    direction = moment_one / FIRST_FIX / (jnp.sqrt(moment_two / SECOND_FIX) + ADAM_EPS)
    return (moment_one[None], moment_two[None], direction[None], user_norm / CLIP_BOUND)


def solution(mesh):
    return jax.shard_map(
        on_device,
        mesh=mesh,
        in_specs=(
            P("dp", None),
            P("dp", None),
            P("dp"),
            P("dp"),
            P("section", None),
            P("section", "dp", None, None),
            P("section", "dp", None, None),
            P("section", "dp", None, None),
        ),
        out_specs=(
            P("section", "dp", None, None),
            P("section", "dp", None, None),
            P("section", "dp", None, None),
            P("dp"),
        ),
        check_vma=False,
    )
```

profile of v0, /device:TPU:0, one launch (start us, length us, event | category | flops | bytes accessed | tf_op | source)
XLA Modules:
  0.0 489.0 jit_solution(7578786689394321223)
XLA Ops:
  7.2 1.8 copy.38
  9.1 2.2 fusion.8
  11.3 48.3 %all-gather.2.cloned.1.call-done = bf16[1,4096,2,256]{3,1,2,0:T(8,128)(2,1)} async-done(((bf16[1,128,2,256]{3,1,2,0:T(8,128)(2,1)}), bf16[1,4096,2,256]{3,1,2,0:T(8,128)(2,1)}) %all-gather.2.cloned.1.call-update) | async-done | bytes 4194320 | tf_op jit(solution)/shard_map/all_gather | solution.py:99
  59.6 2.5 fusion.35
  63.2 3.5 collective-permute-start
  66.8 45.1 %collective-permute-done = bf16[256,4096]{1,0:T(8,128)(2,1)S(1)} collective-permute-done((bf16[256,4096]{1,0:T(8,128)(2,1)S(1)}, bf16[256,4096]{1,0:T(8,128)(2,1)S(1)}, u32[]{:S(2)}, u32[]{:S(2)}) %collective-permute-start) | collective-permute-done | bytes 2097184 | tf_op jit(solution)/shard_map/ppermute | solution.py:21
  114.9 4.5 collective-permute-start.1
  119.5 44.3 %collective-permute-done.1 = bf16[256,4096]{1,0:T(8,128)(2,1)S(1)} collective-permute-done((bf16[256,4096]{1,0:T(8,128)(2,1)S(1)}, bf16[256,4096]{1,0:T(8,128)(2,1)S(1)}, u32[]{:S(2)}, u32[]{:S(2)}) %collective-permute-start.1) | collective-permute-done | bytes 2097184 | tf_op jit(solution)/shard_map/ppermute | solution.py:21
  166.1 2.1 fusion.2
  168.2 5.7 %collective-permute-start.2 = (bf16[256,4096]{1,0:T(8,128)(2,1)}, bf16[256,4096]{1,0:T(8,128)(2,1)}, u32[]{:S(2)}, u32[]{:S(2)}) collective-permute-start(bf16[256,4096]{1,0:T(8,128)(2,1)} %fusion.2), channel_id=1, source_target_pairs={{0,32},{32,64},{64,96},{1,33},{33,65},{65,97},{2,34},{34,66},{66,9... | collective-permute-start | bytes 6291464 | tf_op jit(solution)/shard_map/ppermute | solution.py:21
  174.1 42.4 %collective-permute-done.2 = bf16[256,4096]{1,0:T(8,128)(2,1)} collective-permute-done((bf16[256,4096]{1,0:T(8,128)(2,1)}, bf16[256,4096]{1,0:T(8,128)(2,1)}, u32[]{:S(2)}, u32[]{:S(2)}) %collective-permute-start.2) | collective-permute-done | bytes 2097184 | tf_op jit(solution)/shard_map/ppermute | solution.py:21
  217.4 1.0 fusion.43
  218.5 1.3 copy-done.1
  222.0 2.2 multiply_reduce_fusion.2
  224.2 1.8 subtract_convert_fusion.2
  226.0 1.3 collective-permute-start.3
  227.3 48.1 %collective-permute-done.3 = bf16[256,4096]{1,0:T(8,128)(2,1)S(1)} collective-permute-done((bf16[256,4096]{1,0:T(8,128)(2,1)S(1)}, bf16[256,4096]{1,0:T(8,128)(2,1)S(1)}, u32[]{:S(2)}, u32[]{:S(2)}) %collective-permute-start.3) | collective-permute-done | bytes 2097184 | tf_op jit(solution)/shard_map/ppermute | solution.py:21
  277.1 2.3 subtract_convert_fusion.1
  279.4 1.3 collective-permute-start.4
  280.7 45.2 %collective-permute-done.4 = bf16[256,4096]{1,0:T(8,128)(2,1)S(1)} collective-permute-done((bf16[256,4096]{1,0:T(8,128)(2,1)S(1)}, bf16[256,4096]{1,0:T(8,128)(2,1)S(1)}, u32[]{:S(2)}, u32[]{:S(2)}) %collective-permute-start.4) | collective-permute-done | bytes 2097184 | tf_op jit(solution)/shard_map/ppermute | solution.py:21
  327.6 3.3 subtract_convert_fusion
  330.8 1.5 collective-permute-start.5
  332.8 4.7 select_select_fusion.1
  337.6 39.2 %collective-permute-done.5 = bf16[256,4096]{1,0:T(8,128)(2,1)} collective-permute-done((bf16[256,4096]{1,0:T(8,128)(2,1)}, bf16[256,4096]{1,0:T(8,128)(2,1)}, u32[]{:S(2)}, u32[]{:S(2)}) %collective-permute-start.5) | collective-permute-done | bytes 2097184 | tf_op jit(solution)/shard_map/ppermute | solution.py:21
  376.8 2.4 fusion.29
  379.5 2.3 select_select_fusion
  383.7 8.9 %psum.7 = f32[2]{0:T(128)S(1)} all-reduce(f32[2]{0:T(128)S(1)} %fusion.30), channel_id=1, replica_groups=mesh['section'=4,'dp'=32] {'section'}, use_global_device_ids=true, to_apply=%region_8.9 | all-reduce | flops 2 | bytes 16 | tf_op jit(solution)/shard_map/psum | solution.py:143
  392.8 2.4 fusion.3
  395.2 1.0 fusion.4
  396.2 2.3 pad_maximum_fusion
  399.1 79.3 %reduce-scatter.2.cloned.1.call-done = bf16[128,2,256]{2,0,1:T(8,128)(2,1)} async-done(((bf16[4096,2,256]{2,0,1:T(8,128)(2,1)}), bf16[128,2,256]{2,0,1:T(8,128)(2,1)}) %reduce-scatter.2.cloned.1.call-update) | async-done | bytes 131088 | tf_op jit(solution)/shard_map/reduce_scatter | solution.py:157
  478.4 1.1 divide_bitcast_fusion
  (81 shorter events, 19.0 us)
Async XLA Ops:
  7.2 52.5 %copy-start = (bf16[256,4096]{1,0:T(8,128)(2,1)S(1)}, bf16[256,4096]{1,0:T(8,128)(2,1)}, u32[]{:S(2)}) copy-start(bf16[256,4096]{1,0:T(8,128)(2,1)} %param.8) | copy-start | bytes 6291460
  7.2 52.5 %copy-start.18 = (f32[1,4096]{1,0:T(1,128)S(1)}, f32[1,4096]{1,0:T(1,128)}, u32[]{:S(2)}) copy-start(f32[1,4096]{1,0:T(1,128)} %param.12) | copy-start | bytes 49156
  7.2 52.5 %all-gather.2.cloned.1.call-start = ((), (), s32[]{:S(2)}) async-start(), calls=%async_computation.1 | async-start | bytes 4325376 | tf_op jit(solution)/shard_map/all_gather | solution.py:99
  9.0 469.4 %reduce-scatter.2.cloned.1.call-start = ((), (), s32[]{:S(2)}) async-start(), calls=%async_computation.2 | async-start | bytes 4325376 | tf_op jit(solution)/shard_map/reduce_scatter | solution.py:157
  59.6 2.8 copy-start.13
  63.2 48.7 %collective-permute-start = (bf16[256,4096]{1,0:T(8,128)(2,1)S(1)}, bf16[256,4096]{1,0:T(8,128)(2,1)S(1)}, u32[]{:S(2)}, u32[]{:S(2)}) collective-permute-start(bf16[256,4096]{1,0:T(8,128)(2,1)S(1)} %fusion), channel_id=1, source_target_pairs={{0,32},{32,64},{64,96},{1,33},{33,65},{65,97},{2,34},{34,66},{66,9... | collective-permute-start | bytes 6291464 | tf_op jit(solution)/shard_map/ppermute | solution.py:21
  112.8 1.3 copy-start.4
  114.9 48.8 %collective-permute-start.1 = (bf16[256,4096]{1,0:T(8,128)(2,1)S(1)}, bf16[256,4096]{1,0:T(8,128)(2,1)S(1)}, u32[]{:S(2)}, u32[]{:S(2)}) collective-permute-start(bf16[256,4096]{1,0:T(8,128)(2,1)S(1)} %fusion.1), channel_id=1, source_target_pairs={{0,32},{32,64},{64,96},{1,33},{33,65},{65,97},{2,34},{34,66},{66,9... | collective-permute-start | bytes 6291464 | tf_op jit(solution)/shard_map/ppermute | solution.py:21
  164.7 1.4 copy-start.6
  166.1 7.8 %copy-start.19 = (s32[4]{0:T(128)S(1)}, s32[4]{0:T(128)}, u32[]{:S(2)}) copy-start(s32[4]{0:T(128)} %param.10) | copy-start | bytes 52
  168.2 48.3 %collective-permute-start.2 = (bf16[256,4096]{1,0:T(8,128)(2,1)}, bf16[256,4096]{1,0:T(8,128)(2,1)}, u32[]{:S(2)}, u32[]{:S(2)}) collective-permute-start(bf16[256,4096]{1,0:T(8,128)(2,1)} %fusion.2), channel_id=1, source_target_pairs={{0,32},{32,64},{64,96},{1,33},{33,65},{65,97},{2,34},{34,66},{66,9... | collective-permute-start | bytes 6291464 | tf_op jit(solution)/shard_map/ppermute | solution.py:21
  174.1 43.4 %copy-start.14 = (bf16[1,4096,2,256]{3,1,2,0:T(8,128)(2,1)S(1)}, bf16[1,4096,2,256]{3,1,2,0:T(8,128)(2,1)}, u32[]{:S(2)}) copy-start(bf16[1,4096,2,256]{3,1,2,0:T(8,128)(2,1)} %all-gather.2.cloned.1.call-done) | copy-start | bytes 12582916
  217.4 3.1 copy-start.8
  217.4 2.3 copy-start.1
  219.8 1.6 copy-start.5
  219.8 2.2 copy-start.7
  226.0 49.4 %collective-permute-start.3 = (bf16[256,4096]{1,0:T(8,128)(2,1)S(1)}, bf16[256,4096]{1,0:T(8,128)(2,1)S(1)}, u32[]{:S(2)}, u32[]{:S(2)}) collective-permute-start(bf16[256,4096]{1,0:T(8,128)(2,1)S(1)} %subtract_convert_fusion.2), channel_id=1, source_target_pairs={{32,0},{64,32},{96,64},{33,1},{65,33},{97,65},{34,2},{66,34},{98,6... | collective-permute-start | bytes 6291464 | tf_op jit(solution)/shard_map/ppermute | solution.py:21
  275.4 1.7 copy-start.9
  279.4 46.5 %collective-permute-start.4 = (bf16[256,4096]{1,0:T(8,128)(2,1)S(1)}, bf16[256,4096]{1,0:T(8,128)(2,1)S(1)}, u32[]{:S(2)}, u32[]{:S(2)}) collective-permute-start(bf16[256,4096]{1,0:T(8,128)(2,1)S(1)} %subtract_convert_fusion.1), channel_id=1, source_target_pairs={{32,0},{64,32},{96,64},{33,1},{65,33},{97,65},{34,2},{66,34},{98,6... | collective-permute-start | bytes 6291464 | tf_op jit(solution)/shard_map/ppermute | solution.py:21
  325.9 1.6 copy-start.11
  327.5 4.8 copy-start.20
  330.8 46.0 %collective-permute-start.5 = (bf16[256,4096]{1,0:T(8,128)(2,1)}, bf16[256,4096]{1,0:T(8,128)(2,1)}, u32[]{:S(2)}, u32[]{:S(2)}) collective-permute-start(bf16[256,4096]{1,0:T(8,128)(2,1)} %subtract_convert_fusion), channel_id=1, source_target_pairs={{32,0},{64,32},{96,64},{33,1},{65,33},{97,65},{34,2},{66,34},{98,6... | collective-permute-start | bytes 6291464 | tf_op jit(solution)/shard_map/ppermute | solution.py:21
  332.8 44.0 %copy-start.2 = (bf16[256,4096]{1,0:T(8,128)(2,1)S(1)}, bf16[256,4096]{1,0:T(8,128)(2,1)}, u32[]{:S(2)}) copy-start(bf16[256,4096]{1,0:T(8,128)(2,1)} %param.9) | copy-start | bytes 6291460
  332.8 44.0 %copy-start.15 = (bf16[1,4096,2,256]{3,1,2,0:T(8,128)(2,1)S(1)}, bf16[1,4096,2,256]{3,1,2,0:T(8,128)(2,1)}, u32[]{:S(2)}) copy-start(bf16[1,4096,2,256]{3,1,2,0:T(8,128)(2,1)} %all-gather.2.cloned.1.call-done) | copy-start | bytes 12582916
  337.6 45.0 %copy-start.3 = (bf16[256,4096]{1,0:T(8,128)(2,1)}, bf16[256,4096]{1,0:T(8,128)(2,1)S(1)}, u32[]{:S(2)}) copy-start(bf16[256,4096]{1,0:T(8,128)(2,1)S(1)} %select_select_fusion.1) | copy-start | bytes 6291460
  337.6 41.9 %copy-start.10 = (bf16[256,4096]{1,0:T(8,128)(2,1)S(1)}, bf16[256,4096]{1,0:T(8,128)(2,1)}, u32[]{:S(2)}) copy-start(bf16[256,4096]{1,0:T(8,128)(2,1)} %copy-done.9) | copy-start | bytes 6291460
  337.6 41.9 %copy-start.12 = (bf16[256,4096]{1,0:T(8,128)(2,1)S(1)}, bf16[256,4096]{1,0:T(8,128)(2,1)}, u32[]{:S(2)}) copy-start(bf16[256,4096]{1,0:T(8,128)(2,1)} %copy-done.11) | copy-start | bytes 6291460
  398.5 79.8 %copy-start.16 = (f32[1,128,2,256]{3,2,1,0:T(2,128)S(1)}, f32[1,128,2,256]{3,2,1,0:T(2,128)}, u32[]{:S(2)}) copy-start(f32[1,128,2,256]{3,2,1,0:T(2,128)} %param.14) | copy-start | bytes 786436
  398.5 79.8 %copy-start.17 = (f32[1,128,2,256]{3,2,1,0:T(2,128)S(1)}, f32[1,128,2,256]{3,2,1,0:T(2,128)}, u32[]{:S(2)}) copy-start(f32[1,128,2,256]{3,2,1,0:T(2,128)} %param.15) | copy-start | bytes 786436
Sparse Core Ops, SparseCore 0:
  10.9 48.6 all-gather.1
  398.7 79.6 reduce-scatter.1
where the time goes:
time: 490 us; the launch traced here: 489 us
  waiting for transfers between devices  392 us (80%)
  other arithmetic  23.6 us (5%)
  matrix products  23.1 us (5%)
  starting transfers between devices  17.9 us (4%)
  between operations  14.5 us (3%)
  local copies, waits for them, and re-layouts  8.95 us (2%)
  blocking collectives  8.92 us (2%)
    ppermute x6, waiting for transfers between devices, passed_along(): lax.ppermute(value, axis, [(source, source + steps) for source in range(i...  264 us
    reduce_scatter x1, waiting for transfers between devices, on_device(): lax.psum_scatter(jnp.stack([down_term, up_term], axis=1).astype(jnp.bfloa...  79.3 us
    all_gather x1, waiting for transfers between devices, on_device(): lax.all_gather(weights.astype(jnp.bfloat16), 'dp', axis=1, tiled=True)  48.3 us
    ppermute x6, starting transfers between devices, passed_along(): lax.ppermute(value, axis, [(source, source + steps) for source in range(i...  17.8 us
  transfers between devices with their start and end apart: 8, of which 8 were waited for; matrix products, arithmetic and copies ran while one was open for 2% of the time, Pallas kernels for 0%

commit v1 on v0

--- a/solution.py
+++ b/solution.py
@@ -96,7 +96,20 @@
     block_rows = tok_rows // blocks
     rounds = blocks + section_count - 1
     section_gain = norm_gains[0]
-    packed = lax.all_gather(weights.astype(jnp.bfloat16), "dp", axis=1, tiled=True)
+
+    def _settle_matrix(chunk, comm_axis):
+        tmp = jnp.concatenate(
+            lax.all_to_all(
+                jnp.stack(lax.axis_size(comm_axis) * [chunk], 0),
+                axis_name=comm_axis,
+                split_axis=0,
+                concat_axis=0,
+            ),
+            1,
+        )
+        return tmp
+
+    packed = _settle_matrix(weights.astype(jnp.bfloat16), "dp")
     down_cast = packed[0, :, 0, :]
     up_cast = packed[0, :, 1, :]
     inputs = tokens.reshape(blocks, block_rows, model_width)

time: 490 us -> 504 us (1.029)
  starting transfers between devices: 17.9 us -> 26.5 us
    all_to_all x0 -> x1, waiting for transfers between devices: none -> 51.7 us  [_settle_matrix(): lax.all_to_all(jnp.stack(lax.axis_size(comm_axis) * [chunk], 0), axis_nam...]
    all_gather x1 -> x0, waiting for transfers between devices: 48.3 us -> none  [on_device(): lax.all_gather(weights.astype(jnp.bfloat16), 'dp', axis=1, tiled=True)]
    all_to_all x0 -> x1, starting transfers between devices: none -> 8.54 us  [_settle_matrix(): lax.all_to_all(jnp.stack(lax.axis_size(comm_axis) * [chunk], 0), axis_nam...]
  transfers between devices with their start and end apart: 8 -> 8, of which waited for: 8 -> 8; matrix products, arithmetic and copies ran while one was open for 2% -> 1% of each run, Pallas kernels for 0% -> 0%
where the time goes in v1:
time: 504 us
  waiting for transfers between devices  397 us (79%)
  starting transfers between devices  26.5 us (5%)
  other arithmetic  23.1 us (5%)
  matrix products  21.7 us (4%)
  between operations  14.5 us (3%)
  local copies, waits for them, and re-layouts  11.7 us (2%)
  blocking collectives  8.92 us (2%)
    ppermute x6, waiting for transfers between devices, passed_along(): lax.ppermute(value, axis, [(source, source + steps) for source in range(i...  262 us
    reduce_scatter x1, waiting for transfers between devices, on_device(): lax.psum_scatter(jnp.stack([down_term, up_term], axis=1).astype(jnp.bfloa...  83.4 us
    all_to_all x1, waiting for transfers between devices, _settle_matrix(): lax.all_to_all(jnp.stack(lax.axis_size(comm_axis) * [chunk], 0), axis_nam...  51.7 us
    ppermute x6, starting transfers between devices, passed_along(): lax.ppermute(value, axis, [(source, source + steps) for source in range(i...  17.9 us
  transfers between devices with their start and end apart: 8, of which 8 were waited for; matrix products, arithmetic and copies ran while one was open for 1% of the time, Pallas kernels for 0%

profile of v1, /device:TPU:0, one launch (start us, length us, event | category | flops | bytes accessed | tf_op | source)
XLA Modules:
  0.0 503.7 jit_solution(13215233353865818902)
XLA Ops:
  7.2 1.0 convert_bitcast_fusion
  8.2 2.5 stack.11
  10.7 8.5 %all-to-all-start = ((bf16[32,1,128,2,256]{4,2,3,1,0:T(8,128)(2,1)}), bf16[32,1,128,2,256]{4,2,3,1,0:T(8,128)(2,1)}, u32[]{:S(2)}, u32[]{:S(2)}) async-start(bf16[32,1,128,2,256]{4,2,3,1,0:T(8,128)(2,1)} %stack.11), calls=%async_computation | async-start | bytes 8388608 | tf_op jit(solution)/shard_map/all_to_all | solution.py:102
  20.0 51.7 %all-to-all-done = bf16[32,1,128,2,256]{4,2,3,1,0:T(8,128)(2,1)} async-done(((bf16[32,1,128,2,256]{4,2,3,1,0:T(8,128)(2,1)}), bf16[32,1,128,2,256]{4,2,3,1,0:T(8,128)(2,1)}, u32[]{:S(2)}, u32[]{:S(2)}) %all-to-all-start) | async-done | bytes 4194336 | tf_op jit(solution)/shard_map/all_to_all | solution.py:102
  71.7 2.5 copy.25
  75.8 3.6 collective-permute-start
  79.5 44.8 %collective-permute-done = bf16[256,4096]{1,0:T(8,128)(2,1)S(1)} collective-permute-done((bf16[256,4096]{1,0:T(8,128)(2,1)S(1)}, bf16[256,4096]{1,0:T(8,128)(2,1)S(1)}, u32[]{:S(2)}, u32[]{:S(2)}) %collective-permute-start) | collective-permute-done | bytes 2097184 | tf_op jit(solution)/shard_map/ppermute | solution.py:21
  127.3 4.5 collective-permute-start.1
  131.8 43.9 %collective-permute-done.1 = bf16[256,4096]{1,0:T(8,128)(2,1)S(1)} collective-permute-done((bf16[256,4096]{1,0:T(8,128)(2,1)S(1)}, bf16[256,4096]{1,0:T(8,128)(2,1)S(1)}, u32[]{:S(2)}, u32[]{:S(2)}) %collective-permute-start.1) | collective-permute-done | bytes 2097184 | tf_op jit(solution)/shard_map/ppermute | solution.py:21
  178.1 2.2 fusion.2
  180.2 5.7 %collective-permute-start.2 = (bf16[256,4096]{1,0:T(8,128)(2,1)}, bf16[256,4096]{1,0:T(8,128)(2,1)}, u32[]{:S(2)}, u32[]{:S(2)}) collective-permute-start(bf16[256,4096]{1,0:T(8,128)(2,1)} %fusion.2), channel_id=1, source_target_pairs={{0,32},{32,64},{64,96},{1,33},{33,65},{65,97},{2,34},{34,66},{66,9... | collective-permute-start | bytes 6291464 | tf_op jit(solution)/shard_map/ppermute | solution.py:21
  186.1 42.0 %collective-permute-done.2 = bf16[256,4096]{1,0:T(8,128)(2,1)} collective-permute-done((bf16[256,4096]{1,0:T(8,128)(2,1)}, bf16[256,4096]{1,0:T(8,128)(2,1)}, u32[]{:S(2)}, u32[]{:S(2)}) %collective-permute-start.2) | collective-permute-done | bytes 2097184 | tf_op jit(solution)/shard_map/ppermute | solution.py:21
  230.2 1.2 copy-done.1
  233.6 2.2 multiply_reduce_fusion.2
  235.8 1.8 subtract_convert_fusion.2
  237.7 1.3 collective-permute-start.3
  239.0 47.8 %collective-permute-done.3 = bf16[256,4096]{1,0:T(8,128)(2,1)S(1)} collective-permute-done((bf16[256,4096]{1,0:T(8,128)(2,1)S(1)}, bf16[256,4096]{1,0:T(8,128)(2,1)S(1)}, u32[]{:S(2)}, u32[]{:S(2)}) %collective-permute-start.3) | collective-permute-done | bytes 2097184 | tf_op jit(solution)/shard_map/ppermute | solution.py:21
  288.4 2.3 subtract_convert_fusion.1
  290.7 1.3 collective-permute-start.4
  292.0 44.8 %collective-permute-done.4 = bf16[256,4096]{1,0:T(8,128)(2,1)S(1)} collective-permute-done((bf16[256,4096]{1,0:T(8,128)(2,1)S(1)}, bf16[256,4096]{1,0:T(8,128)(2,1)S(1)}, u32[]{:S(2)}, u32[]{:S(2)}) %collective-permute-start.4) | collective-permute-done | bytes 2097184 | tf_op jit(solution)/shard_map/ppermute | solution.py:21
  338.5 3.3 subtract_convert_fusion
  341.8 1.5 collective-permute-start.5
  343.7 4.7 select_select_fusion.1
  348.5 38.9 %collective-permute-done.5 = bf16[256,4096]{1,0:T(8,128)(2,1)} collective-permute-done((bf16[256,4096]{1,0:T(8,128)(2,1)}, bf16[256,4096]{1,0:T(8,128)(2,1)}, u32[]{:S(2)}, u32[]{:S(2)}) %collective-permute-start.5) | collective-permute-done | bytes 2097184 | tf_op jit(solution)/shard_map/ppermute | solution.py:21
  387.4 2.4 fusion.29
  390.1 2.3 select_select_fusion
  394.3 8.9 %psum.7 = f32[2]{0:T(128)S(1)} all-reduce(f32[2]{0:T(128)S(1)} %fusion.30), channel_id=1, replica_groups=mesh['section'=4,'dp'=32] {'section'}, use_global_device_ids=true, to_apply=%region_8.9 | all-reduce | flops 2 | bytes 16 | tf_op jit(solution)/shard_map/psum | solution.py:156
  403.3 2.4 fusion.3
  405.7 1.0 fusion.4
  406.8 2.3 pad_maximum_fusion
  409.6 83.4 %reduce-scatter.2.cloned.1.call-done = bf16[128,2,256]{2,0,1:T(8,128)(2,1)} async-done(((bf16[4096,2,256]{2,0,1:T(8,128)(2,1)}), bf16[128,2,256]{2,0,1:T(8,128)(2,1)}) %reduce-scatter.2.cloned.1.call-update) | async-done | bytes 131088 | tf_op jit(solution)/shard_map/reduce_scatter | solution.py:170
  493.1 1.1 divide_bitcast_fusion
  (83 shorter events, 21.2 us)
Async XLA Ops:
  10.7 8.6 %copy-start = (bf16[256,4096]{1,0:T(8,128)(2,1)S(1)}, bf16[256,4096]{1,0:T(8,128)(2,1)}, u32[]{:S(2)}) copy-start(bf16[256,4096]{1,0:T(8,128)(2,1)} %param.8) | copy-start | bytes 6291460
  10.7 61.0 %all-to-all-start = ((bf16[32,1,128,2,256]{4,2,3,1,0:T(8,128)(2,1)}), bf16[32,1,128,2,256]{4,2,3,1,0:T(8,128)(2,1)}, u32[]{:S(2)}, u32[]{:S(2)}) async-start(bf16[32,1,128,2,256]{4,2,3,1,0:T(8,128)(2,1)} %stack.11), calls=%async_computation | async-start | bytes 8388608 | tf_op jit(solution)/shard_map/all_to_all | solution.py:102
  19.2 473.8 %reduce-scatter.2.cloned.1.call-start = ((), (), s32[]{:S(2)}) async-start(), calls=%async_computation.2 | async-start | bytes 4325376 | tf_op jit(solution)/shard_map/reduce_scatter | solution.py:170
  20.0 54.2 %copy-start.18 = (f32[1,4096]{1,0:T(1,128)S(1)}, f32[1,4096]{1,0:T(1,128)}, u32[]{:S(2)}) copy-start(f32[1,4096]{1,0:T(1,128)} %param.12) | copy-start | bytes 49156
  74.2 103.4 %copy-start.4 = (bf16[32,1,128,2,256]{4,2,0,3,1:T(8,128)(2,1)}, bf16[32,1,128,2,256]{4,2,0,3,1:T(8,128)(2,1)S(1)}, u32[]{:S(2)}) copy-start(bf16[32,1,128,2,256]{4,2,0,3,1:T(8,128)(2,1)S(1)} %copy.25) | copy-start | bytes 12582916
  75.8 48.4 %collective-permute-start = (bf16[256,4096]{1,0:T(8,128)(2,1)S(1)}, bf16[256,4096]{1,0:T(8,128)(2,1)S(1)}, u32[]{:S(2)}, u32[]{:S(2)}) collective-permute-start(bf16[256,4096]{1,0:T(8,128)(2,1)S(1)} %fusion), channel_id=1, source_target_pairs={{0,32},{32,64},{64,96},{1,33},{33,65},{65,97},{2,34},{34,66},{66,9... | collective-permute-start | bytes 6291464 | tf_op jit(solution)/shard_map/ppermute | solution.py:21
  125.2 1.3 copy-start.7
  127.3 48.4 %collective-permute-start.1 = (bf16[256,4096]{1,0:T(8,128)(2,1)S(1)}, bf16[256,4096]{1,0:T(8,128)(2,1)S(1)}, u32[]{:S(2)}, u32[]{:S(2)}) collective-permute-start(bf16[256,4096]{1,0:T(8,128)(2,1)S(1)} %fusion.1), channel_id=1, source_target_pairs={{0,32},{32,64},{64,96},{1,33},{33,65},{65,97},{2,34},{34,66},{66,9... | collective-permute-start | bytes 6291464 | tf_op jit(solution)/shard_map/ppermute | solution.py:21
  176.7 1.3 copy-start.9
  178.0 7.9 %copy-start.19 = (s32[4]{0:T(128)S(1)}, s32[4]{0:T(128)}, u32[]{:S(2)}) copy-start(s32[4]{0:T(128)} %param.10) | copy-start | bytes 52
  180.2 47.9 %collective-permute-start.2 = (bf16[256,4096]{1,0:T(8,128)(2,1)}, bf16[256,4096]{1,0:T(8,128)(2,1)}, u32[]{:S(2)}, u32[]{:S(2)}) collective-permute-start(bf16[256,4096]{1,0:T(8,128)(2,1)} %fusion.2), channel_id=1, source_target_pairs={{0,32},{32,64},{64,96},{1,33},{33,65},{65,97},{2,34},{34,66},{66,9... | collective-permute-start | bytes 6291464 | tf_op jit(solution)/shard_map/ppermute | solution.py:21
  186.1 43.0 %copy-start.5 = (bf16[32,1,128,2,256]{4,2,0,3,1:T(8,128)(2,1)S(1)}, bf16[32,1,128,2,256]{4,2,0,3,1:T(8,128)(2,1)}, u32[]{:S(2)}) copy-start(bf16[32,1,128,2,256]{4,2,0,3,1:T(8,128)(2,1)} %copy-done.4) | copy-start | bytes 12582916
  229.1 3.1 copy-start.11
  229.1 2.3 copy-start.1
  231.4 1.6 copy-start.8
  231.4 2.2 copy-start.10
  237.7 49.1 %collective-permute-start.3 = (bf16[256,4096]{1,0:T(8,128)(2,1)S(1)}, bf16[256,4096]{1,0:T(8,128)(2,1)S(1)}, u32[]{:S(2)}, u32[]{:S(2)}) collective-permute-start(bf16[256,4096]{1,0:T(8,128)(2,1)S(1)} %subtract_convert_fusion.2), channel_id=1, source_target_pairs={{32,0},{64,32},{96,64},{33,1},{65,33},{97,65},{34,2},{66,34},{98,6... | collective-permute-start | bytes 6291464 | tf_op jit(solution)/shard_map/ppermute | solution.py:21
  286.7 1.6 copy-start.12
  290.7 46.1 %collective-permute-start.4 = (bf16[256,4096]{1,0:T(8,128)(2,1)S(1)}, bf16[256,4096]{1,0:T(8,128)(2,1)S(1)}, u32[]{:S(2)}, u32[]{:S(2)}) collective-permute-start(bf16[256,4096]{1,0:T(8,128)(2,1)S(1)} %subtract_convert_fusion.1), channel_id=1, source_target_pairs={{32,0},{64,32},{96,64},{33,1},{65,33},{97,65},{34,2},{66,34},{98,6... | collective-permute-start | bytes 6291464 | tf_op jit(solution)/shard_map/ppermute | solution.py:21
  336.8 1.7 copy-start.14
  338.5 4.8 copy-start.20
  341.8 45.6 %collective-permute-start.5 = (bf16[256,4096]{1,0:T(8,128)(2,1)}, bf16[256,4096]{1,0:T(8,128)(2,1)}, u32[]{:S(2)}, u32[]{:S(2)}) collective-permute-start(bf16[256,4096]{1,0:T(8,128)(2,1)} %subtract_convert_fusion), channel_id=1, source_target_pairs={{32,0},{64,32},{96,64},{33,1},{65,33},{97,65},{34,2},{66,34},{98,6... | collective-permute-start | bytes 6291464 | tf_op jit(solution)/shard_map/ppermute | solution.py:21
  343.7 43.7 %copy-start.2 = (bf16[256,4096]{1,0:T(8,128)(2,1)S(1)}, bf16[256,4096]{1,0:T(8,128)(2,1)}, u32[]{:S(2)}) copy-start(bf16[256,4096]{1,0:T(8,128)(2,1)} %param.9) | copy-start | bytes 6291460
  343.7 43.7 %copy-start.6 = (bf16[32,1,128,2,256]{4,2,0,3,1:T(8,128)(2,1)S(1)}, bf16[32,1,128,2,256]{4,2,0,3,1:T(8,128)(2,1)}, u32[]{:S(2)}) copy-start(bf16[32,1,128,2,256]{4,2,0,3,1:T(8,128)(2,1)} %copy-done.4) | copy-start | bytes 12582916
  348.5 44.7 %copy-start.3 = (bf16[256,4096]{1,0:T(8,128)(2,1)}, bf16[256,4096]{1,0:T(8,128)(2,1)S(1)}, u32[]{:S(2)}) copy-start(bf16[256,4096]{1,0:T(8,128)(2,1)S(1)} %select_select_fusion.1) | copy-start | bytes 6291460
  348.5 41.6 %copy-start.13 = (bf16[256,4096]{1,0:T(8,128)(2,1)S(1)}, bf16[256,4096]{1,0:T(8,128)(2,1)}, u32[]{:S(2)}) copy-start(bf16[256,4096]{1,0:T(8,128)(2,1)} %copy-done.12) | copy-start | bytes 6291460
  348.5 41.6 %copy-start.15 = (bf16[256,4096]{1,0:T(8,128)(2,1)S(1)}, bf16[256,4096]{1,0:T(8,128)(2,1)}, u32[]{:S(2)}) copy-start(bf16[256,4096]{1,0:T(8,128)(2,1)} %copy-done.14) | copy-start | bytes 6291460
  409.1 84.0 %copy-start.16 = (f32[1,128,2,256]{3,2,1,0:T(2,128)S(1)}, f32[1,128,2,256]{3,2,1,0:T(2,128)}, u32[]{:S(2)}) copy-start(f32[1,128,2,256]{3,2,1,0:T(2,128)} %param.14) | copy-start | bytes 786436
  409.1 84.0 %copy-start.17 = (f32[1,128,2,256]{3,2,1,0:T(2,128)S(1)}, f32[1,128,2,256]{3,2,1,0:T(2,128)}, u32[]{:S(2)}) copy-start(f32[1,128,2,256]{3,2,1,0:T(2,128)} %param.15) | copy-start | bytes 786436
Sparse Core Ops, SparseCore 0:
  409.2 83.7 reduce-scatter.1
